TPU v7x, 32 devices: a whole 2x2x4 slice. The times are simulated.
32 devices in a mesh: tm: 8 (over z, x), exp: 4 (over y, core).
Axes of the slice: x: 2, y: 2, z: 4, core: 2. Of those that a mesh axis runs over, the one named last changes fastest.
Arguments:
- transitions: float32 [512, 256, 256], P('tm'), may hold values from -0.2 to 1.2
- pattern: int32 [512, 4, 4], P('tm'), may hold values from 0 to 1, as said below
- obs_mask: int32 [4, 512, 256], P('exp', 'tm'), may hold values 0 or 1
- measured: float32 [4, 512, 256], P('exp', 'tm'), may hold values from -6 to 6
- prior_mean: float32 [4, 256], P('exp'), may hold values from -6 to 6
- filter_gain: float32 [256], replicated, may hold values from 0 to 0.6
- smooth_gain: float32 [256], replicated, may hold values from 0.3 to 1
Outputs:
- smoothed: float32 [4, 512, 256], P('exp', 'tm')
- information: float32 [256, 256], replicated
Inputs may be any that keep to these rules, and one draw needn't show every extreme that they name: `pattern`: diagonal blocks are always present.
All inputs are finite; a program needn't handle non-finite values. No bound on the sum of `obs_mask` on one device may be relied on, other than what follows from the above.
Results may differ from a plain program's by a relative error of at most 0.0001.
Values sent between devices are 32-bit elements; how exact they have to be, the bound alone decides.
A program may use at most 192 MiB of HBM per device.

v0:
```python
import jax
import jax.numpy as jnp
from jax import lax
from jax.sharding import PartitionSpec as P


def entering(x, axis, combine, identity, reverse):
    length, index = (lax.axis_size(axis), lax.axis_index(axis))
    everything = jax.tree.map(lambda part: lax.all_gather(part, axis), x)
    start = jax.tree.map(
        lambda part, zero: jnp.broadcast_to(jnp.asarray(zero, part.dtype), part.shape), x, identity
    )

    def hop(k, before):
        at = length - 1 - k if reverse else k
        reached = at > index if reverse else at < index
        new = combine(before, jax.tree.map(lambda part: part[at], everything))
        return jax.tree.map(lambda a, b: jnp.where(reached, a, b), new, before)

    return lax.fori_loop(0, length, hop, start)


def masked_dense(transitions, pattern):
    count_steps, state_width, _ = transitions.shape
    block_count = pattern.shape[1]
    block_size = state_width // block_count
    reshaped = transitions.reshape(count_steps, block_count, block_size, block_count, block_size)
    weights = pattern.astype(jnp.float32)[:, :, None, :, None]
    return (reshaped * weights).reshape(count_steps, state_width, state_width)


def chain_product(matrices):
    while matrices.shape[0] > 1:
        paired = matrices.shape[0] // 2 * 2
        earlier_maps = matrices[0:paired:2]
        later_maps = matrices[1:paired:2]
        joined = jnp.einsum(
            "bij,bjk->bik", later_maps, earlier_maps, precision=lax.Precision.HIGHEST
        )
        matrices = joined
    return matrices[0]


def compose(earlier_maps, later_maps):
    highest = lax.Precision.HIGHEST
    return (
        jnp.dot(later_maps[0], earlier_maps[0], precision=highest),
        jnp.dot(later_maps[0], earlier_maps[1], precision=highest) + later_maps[1],
    )


def run_filter(dense_steps, keep_rows, drive_terms, start_state):

    def update(state, inputs):
        trans_step, keep_step, drive_step = inputs
        predict = jnp.dot(trans_step, state, precision=lax.Precision.HIGHEST)
        state = keep_step * predict + drive_step
        return (state, (state, predict))

    last_state, (filtered, predicted) = lax.scan(
        update, start_state, (dense_steps, keep_rows, drive_terms)
    )
    return (last_state, filtered, predicted)


def run_smoother(dense_steps, filtered, predicted, smooth_gain, carried_in):

    def update(carried, inputs):
        trans_step, state, predict = inputs
        smooth_now = state + smooth_gain * carried
        residual = smooth_now - predict
        carried = jnp.dot(residual, trans_step, precision=lax.Precision.HIGHEST)
        return (carried, (smooth_now, residual))

    first_carry, (smoothed, residuals) = lax.scan(
        update, carried_in, (dense_steps, filtered, predicted), reverse=True
    )
    return (first_carry, smoothed, residuals)


def shards(transitions, pattern, obs_mask, measured, prior_mean, filter_gain, smooth_gain):
    highest = lax.Precision.HIGHEST
    dense_steps = masked_dense(transitions, pattern)
    state_width = dense_steps.shape[1]
    count_steps = dense_steps.shape[0]
    mask_rows = obs_mask[0].astype(jnp.float32)
    keep_rows = 1.0 - filter_gain[None, :] * mask_rows
    drive_terms = filter_gain[None, :] * mask_rows * measured[0]
    filter_map = chain_product(keep_rows[:, :, None] * dense_steps)
    smoother_map = chain_product(smooth_gain[None, :, None] * dense_steps).T
    zero_vector = jnp.zeros((state_width,), jnp.float32)
    filter_shift, _, _ = run_filter(dense_steps, keep_rows, drive_terms, zero_vector)
    prior_state = prior_mean[0]
    identity = jnp.eye(state_width, dtype=jnp.float32)
    prefix_maps = entering(
        (filter_map, filter_shift), "tm", compose, (identity, zero_vector), False
    )
    start_state = jnp.dot(prefix_maps[0], prior_state, precision=highest) + prefix_maps[1]
    _, filtered, predicted = run_filter(dense_steps, keep_rows, drive_terms, start_state)
    smoother_shift, _, _ = run_smoother(dense_steps, filtered, predicted, smooth_gain, zero_vector)
    suffix_maps = entering(
        (smoother_map, smoother_shift), "tm", compose, (identity, zero_vector), True
    )
    carried_in = suffix_maps[1]
    _, smoothed, residuals = run_smoother(dense_steps, filtered, predicted, smooth_gain, carried_in)
    local_info = jnp.dot(residuals.T, residuals, precision=highest)
    total_info = lax.psum(local_info, ("tm", "exp"))
    information = total_info / (count_steps * lax.axis_size("tm") * lax.axis_size("exp"))
    return (smoothed[None], information)


def solution(mesh):
    in_specs = (
        P("tm", None, None),
        P("tm", None, None),
        P("exp", "tm", None),
        P("exp", "tm", None),
        P("exp", None),
        P(),
        P(),
    )
    out_specs = (P("exp", "tm", None), P())
    return jax.shard_map(shards, mesh=mesh, in_specs=in_specs, out_specs=out_specs, check_vma=False)
```

profile of v0, /device:TPU:0, one launch (start us, length us, event | category | flops | bytes accessed | tf_op | source)
XLA Modules:
  0.0 665.8 jit_solution(17805602499832563561)
XLA Ops:
  8.1 11.2 %mul.71 = f32[64,4,64,4,64]{4,3,2,1,0:T(4,128)} broadcast(f32[64,4,4]{2,1,0:T(4,128)S(1)} %copy.10), dimensions={0,1,3} | broadcast | bytes 16781312 | tf_op jit(solution)/shard_map/mul | solution.py:29
  19.3 30.5 %mul.72 = f32[64,256,256]{2,1,0:T(8,128)} reshape(f32[64,4,64,4,64]{4,3,2,1,0:T(4,128)} %mul.71) | data formatting | bytes 33554432 | tf_op jit(solution)/shard_map/mul | solution.py:29
  49.8 17.7 %broadcast_multiply_fusion = (f32[64,256,256]{2,1,0:T(8,128)S(1)}, f32[64,256,256]{2,1,0:T(8,128)}) fusion(f32[64,256]{1,0:T(8,128)S(1)} %get-tuple-element.1043, f32[64,256,256]{2,1,0:T(8,128)} %param.19, f32[64,256,256]{2,1,0:T(8,128)} %mul.72), kind=kLoop, calls=%fused_computation.50 | loop fusion | flops 8388608 | bytes 67174400 | tf_op jit(solution)/shard_map/mul | solution.py:89
  67.6 10.7 %fusion.27 = f32[32,256,256]{2,1,0:T(8,128)} fusion(f32[64,256,256]{2,1,0:T(8,128)S(1)} %get-tuple-element.734), kind=kOutput, calls=%fused_computation.47 | convolution fusion | flops 6442450944 | bytes 25165824 | tf_op jit(solution)/shard_map/bij,bjk->bik/dot_general | solution.py:37
  78.2 8.4 %fusion.33 = f32[16,256,256]{2,1,0:T(8,128)S(1)} fusion(f32[32,256,256]{2,1,0:T(8,128)} %fusion.27), kind=kOutput, calls=%fused_computation.55 | convolution fusion | flops 3221225472 | bytes 12582912 | tf_op jit(solution)/shard_map/bij,bjk->bik/dot_general | solution.py:37
  86.7 2.2 fusion.39
  91.9 7.3 %broadcast_multiply_fusion.1 = f32[64,256,256]{2,1,0:T(8,128)S(1)} fusion(f32[64,256,256]{2,1,0:T(8,128)} %get-tuple-element.1124, f32[256]{0:T(256)S(1)} %copy-done.1), kind=kLoop, calls=%fused_computation.54 | loop fusion | flops 4194304 | bytes 33555456 | tf_op jit(solution)/shard_map/mul | solution.py:90
  99.1 10.7 %fusion.30 = f32[32,256,256]{2,1,0:T(8,128)} fusion(f32[64,256,256]{2,1,0:T(8,128)S(1)} %broadcast_multiply_fusion.1), kind=kOutput, calls=%fused_computation.51 | convolution fusion | flops 6442450944 | bytes 25165824 | tf_op jit(solution)/shard_map/bij,bjk->bik/dot_general | solution.py:37
  109.8 8.5 %fusion.36 = f32[16,256,256]{2,1,0:T(8,128)S(1)} fusion(f32[32,256,256]{2,1,0:T(8,128)} %fusion.30), kind=kOutput, calls=%fused_computation.58 | convolution fusion | flops 3221225472 | bytes 12582912 | tf_op jit(solution)/shard_map/bij,bjk->bik/dot_general | solution.py:37
  118.3 2.2 fusion.42
  122.3 1.3 fusion.58
  123.8 85.5 %while.92 = (s32[]{:T(128)}, f32[256]{0:T(256)S(1)}, f32[64,256]{1,0:T(8,128)S(1)}, f32[64,256,256]{2,1,0:T(8,128)}, f32[64,256]{1,0:T(8,128)S(1)}, /*index=5*/s32[]{:T(128)}, s32[]{:T(128)}) while((s32[]{:T(128)}, f32[256]{0:T(256)S(1)}, f32[64,256]{1,0:T(8,128)S(1)}, f32[64,256,256]{2,1,0:T(8,128)}, f32[64,256]{1,0:T(8,128)S(1)}, ...), condition=%wide.region_1.2_spmd.clone, body=%wide.region_0.1_spmd.clone.sunk | while | flops 787203 | bytes 275035 | solution.py:60
  125.1 1.2 fusion.108
  126.5 1.2 fusion.108
  127.8 1.2 fusion.108
  129.1 1.2 fusion.108
  130.5 1.2 fusion.108
  135.8 1.2 fusion.108
  137.1 1.2 fusion.108
  138.5 1.2 fusion.108
  139.8 1.2 fusion.108
  142.5 1.3 fusion.108
  145.1 1.2 fusion.108
  146.5 1.2 fusion.108
  147.8 1.3 fusion.108
  149.1 1.3 fusion.108
  151.8 1.2 fusion.108
  153.2 1.2 fusion.108
  154.5 1.2 fusion.108
  155.8 1.2 fusion.108
  157.2 1.2 fusion.108
  158.5 1.2 fusion.108
  159.8 1.2 fusion.108
  161.2 1.2 fusion.108
  163.8 1.2 fusion.108
  165.2 1.3 fusion.108
  166.5 1.3 fusion.108
  167.9 1.3 fusion.108
  169.2 1.3 fusion.108
  170.5 1.2 fusion.108
  171.9 1.2 fusion.108
  177.2 1.2 fusion.108
  178.5 1.2 fusion.108
  179.9 1.2 fusion.108
  185.2 1.2 fusion.108
  186.5 1.2 fusion.108
  187.9 1.2 fusion.108
  209.2 22.2 %all-gather.4 = f32[8,1,256]{2,1,0:T(1,128)S(1)} all-gather(f32[1,1,256]{2,1,0:T(1,128)S(1)} %bitcast.198), channel_id=4, replica_groups=mesh['tm'=8,'exp'=4] {'tm'}, dimensions={0}, use_global_device_ids=true | all-gather | bytes 9216 | tf_op jit(solution)/shard_map/all_gather | solution.py:9
  231.5 21.6 %while.93 = (s32[]{:T(128)}, f32[256,256]{1,0:T(8,128)S(1)}, f32[256]{0:T(256)S(1)}, s32[]{:T(128)}, f32[8,256,256]{2,1,0:T(8,128)}, /*index=5*/f32[8,256]{1,0:T(8,128)S(1)}, s32[]{:T(128)}, s32[]{:T(128)}) while((s32[]{:T(128)}, f32[256,256]{1,0:T(8,128)S(1)}, f32[256]{0:T(256)S(1)}, s32[]{:T(128)}, f32[8,256,256]{2,1,0:T(8,128)}, ...), condition=%wide.region_3.4_spmd.clone, body=%wide.region_2.3_spmd.clone.sunk | while | flops 202179584 | bytes 1846383 | solution.py:20
  232.8 1.3 convolution_select_fusion.2
  235.5 1.3 convolution_select_fusion.2
  238.2 1.3 convolution_select_fusion.2
  240.9 1.3 convolution_select_fusion.2
  243.6 1.3 convolution_select_fusion.2
  246.3 1.3 convolution_select_fusion.2
  249.0 1.3 convolution_select_fusion.2
  251.7 1.3 convolution_select_fusion.2
  253.5 90.9 %while.89 = (s32[]{:T(128)}, f32[256]{0:T(256)S(1)}, f32[64,256]{1,0:T(8,128)S(1)}, f32[64,256]{1,0:T(8,128)S(1)}, f32[64,256]{1,0:T(8,128)S(1)}, /*index=5*/f32...) while((s32[]{:T(128)}, f32[256]{0:T(256)S(1)}, f32[64,256]{1,0:T(8,128)S(1)}, ...), condition=%wide.region_5.6_spmd, body=%wide.region_4.5_spmd.sunk | while | flops 786946 | bytes 277097 | solution.py:60
  344.4 77.4 %while.90 = (s32[]{:T(128)}, f32[256]{0:T(256)S(1)}, f32[64,256]{1,0:T(8,128)S(1)}, f32[256]{0:T(256)S(1)}, f32[64,256]{1,0:T(8,128)S(1)}, /*index=5*/f32[64,256,256]{2,1,0:T(8,128)}, s32[]{:T(128)}, s32[]{:T(128)}) while((s32[]{:T(128)}, f32[256]{0:T(256)S(1)}, f32[64,256]{1,0:T(8,128)S(1)}, f32[256]{0:T(256)S(1)}, f32[64,256]{1,0:T(8,128)S(1)}, ...), condition=%wide.region_7.8_spmd, body=%wide.region_6.7_spmd.sunk | while | flops 787203 | bytes 273513 | solution.py:75
  421.8 16.3 %all-gather.5 = f32[8,1,256]{2,1,0:T(1,128)S(1)} all-gather(f32[1,1,256]{2,1,0:T(1,128)S(1)} %bitcast.197), channel_id=5, replica_groups=mesh['tm'=8,'exp'=4] {'tm'}, dimensions={0}, use_global_device_ids=true | all-gather | bytes 9216 | tf_op jit(solution)/shard_map/all_gather | solution.py:9
  438.1 10.8 %while.94 = (s32[]{:T(128)}, f32[256]{0:T(256)S(1)}, s32[]{:T(128)}, f32[8,256,256]{2,1,0:T(8,128)}, f32[8,256]{1,0:T(8,128)S(1)}, /*index=5*/s32[]{:T(128)}, s32[]{:T(128)}, s32[]{:T(128)}, s32[]{:T(128)}) while((s32[]{:T(128)}, f32[256]{0:T(256)S(1)}, s32[]{:T(128)}, f32[8,256,256]{2,1,0:T(8,128)}, f32[8,256]{1,0:T(8,128)S(1)}, ...), condition=%wide.region_9.10_spmd.clone, body=%wide.region_8.9_spmd.clone.sunk | while | flops 787464 | bytes 272552 | solution.py:20
  448.9 83.7 %while.91 = (s32[]{:T(128)}, f32[256]{0:T(256)S(1)}, f32[64,256]{1,0:T(8,128)S(1)}, f32[64,256]{1,0:T(8,128)S(1)}, f32[64,256]{1,0:T(8,128)S(1)}, /*index=5*/f32...) while((s32[]{:T(128)}, f32[256]{0:T(256)S(1)}, ...), condition=%wide.region_11.12_spmd, body=%wide.region_10.11_spmd.sunk | while | flops 787203 | bytes 278665 | solution.py:75
  533.7 123.9 %all-reduce.2.cloned.1.call-done = f32[256,256]{1,0:T(8,128)} async-done(((f32[256,256]{1,0:T(8,128)}), f32[256,256]{1,0:T(8,128)}) %all-reduce.2.cloned.1.call-update) | async-done | bytes 262160 | tf_op jit(solution)/shard_map/psum | solution.py:107
  657.6 1.7 broadcast_multiply_fusion.2
  (1167 shorter events, 313.4 us)
Async XLA Ops:
  7.2 245.9 %copy-start = (f32[1,256]{1,0:T(1,128)S(1)}, f32[1,256]{1,0:T(1,128)}, u32[]{:S(2)}) copy-start(f32[1,256]{1,0:T(1,128)} %param.23) | copy-start | bytes 3076
  7.2 224.3 %all-gather.11.cloned.1.call-start = ((), (), s32[]{:S(2)}) async-start(), calls=%async_computation.2 | async-start | bytes 2359296 | tf_op jit(solution)/shard_map/all_gather | solution.py:9
  19.3 30.5 %copy-start.3 = (f32[1,64,256]{2,1,0:T(8,128)S(1)}, f32[1,64,256]{2,1,0:T(8,128)}, u32[]{:S(2)}) copy-start(f32[1,64,256]{2,1,0:T(8,128)} %param.22) | copy-start | bytes 196612
  19.3 30.5 %copy-start.4 = (s32[1,64,256]{2,1,0:T(8,128)S(1)}, s32[1,64,256]{2,1,0:T(8,128)}, u32[]{:S(2)}) copy-start(s32[1,64,256]{2,1,0:T(8,128)} %param.21) | copy-start | bytes 196612
  19.3 30.5 %copy-start.5 = (f32[256]{0:T(256)S(1)}, f32[256]{0:T(256)}, u32[]{:S(2)}) copy-start(f32[256]{0:T(256)} %param.24) | copy-start | bytes 3076
  86.6 5.2 copy-start.1
  91.8 346.3 %all-gather.9.cloned.1.call-start = ((), (), s32[]{:S(2)}) async-start(), calls=%async_computation.1 | async-start | bytes 2359296 | tf_op jit(solution)/shard_map/all_gather | solution.py:9
  123.6 534.0 %all-reduce.2.cloned.1.call-start = ((), (), s32[]{:S(2)}) async-start(), calls=%async_computation | async-start | bytes 524288 | tf_op jit(solution)/shard_map/psum | solution.py:107
  532.6 126.7 %copy-start.2 = (f32[64,256]{1,0:T(8,128)}, f32[64,256]{1,0:T(8,128)S(1)}, u32[]{:S(2)}) copy-start(f32[64,256]{1,0:T(8,128)S(1)} %get-tuple-element.599) | copy-start | bytes 196612
Sparse Core Ops, SparseCore 0:
  91.9 52.1 all-gather.10
  146.8 47.8 all-gather.8
  533.9 123.7 all-reduce.1
where the time goes:
time: 676 us; the launch traced here: 666 us
  matrix products  383 us (57%)
  waiting for transfers between devices  124 us (18%)
  local copies, waits for them, and re-layouts  63 us (9%)
  blocking collectives  38.6 us (6%)
  other arithmetic  33 us (5%)
  between operations  14 us (2%)
  loops' own time  9.82 us (1%)
    dot_general x128, matrix products, update(): predict = jnp.dot(trans_step, state, precision=lax.Precision.HIGHEST)  157 us
    dot_general x128, matrix products, update(): carried = jnp.dot(residual, trans_step, precision=lax.Precision.HIGHEST)  146 us
    psum x1, waiting for transfers between devices, shards(): total_info = lax.psum(local_info, ('tm', 'exp'))  124 us
    dot_general x12, matrix products, chain_product(): jnp.einsum('bij,bjk->bik', later_maps, earlier_maps, precision=lax.Precis...  48.6 us
    mul x2, local copies, waits for them, and re-layouts, masked_dense(): return (reshaped * weights).reshape(count_steps, state_width, state_width)  41.7 us
    all_gather x2, blocking collectives, entering(): everything = jax.tree.map(lambda part: lax.all_gather(part, axis), x)  38.6 us
    dot_general x16, matrix products, compose(): jnp.dot(later_maps[0], earlier_maps[1], precision=highest) + later_maps[1]  19.6 us
    mul x1, other arithmetic, shards(): filter_map = chain_product(keep_rows[:, :, None] * dense_steps)  17.7 us
  transfers between devices with their start and end apart: 3, of which 1 were waited for; matrix products, arithmetic and copies ran while one was open for 45% of the time, Pallas kernels for 0%

commit v1 on v0

v1 whole, which is shorter than its diff:
```python
import functools

import jax
import jax.numpy as jnp
from jax import lax
from jax.experimental import pallas as pl
from jax.experimental.pallas import tpu as pltpu
from jax.sharding import PartitionSpec as P

HIGHEST = lax.Precision.HIGHEST
LANES = 128
SUB = 8
CHUNKS = 8
VMEM_BYTES = 60 * 1024 * 1024


def split(x):
    high = x.astype(jnp.bfloat16)
    low = (x - high.astype(jnp.float32)).astype(jnp.bfloat16)
    return high, low


def dot_rhs_t(a, b):
    return lax.dot_general(a, b, (((1,), (1,)), ((), ())), preferred_element_type=jnp.float32)


def to_column(row):
    width = row.shape[1]
    padded = jnp.concatenate([row, jnp.zeros((LANES - SUB, width), jnp.float32)], axis=0)
    return padded.T


def chain_kernel(pattern_ref, trans_ref, obs_ref, meas_ref, fgain_ref, sgain_ref,
                 dense_ref, apre_ref, bpre_ref, pmap_ref, ptot_ref, gain_ref, drive_ref, state, pre):
    j, c = pl.program_id(0), pl.program_id(1)
    length, chunks = pl.num_programs(0), pl.num_programs(1)
    t = c * length + j
    width = trans_ref.shape[-1]
    blocks = 4
    block = width // blocks
    lane = lax.broadcasted_iota(jnp.int32, (1, width), 1) // block
    pieces = []
    for i in range(blocks):
        weights = jnp.zeros((1, width), jnp.float32)
        for k in range(blocks):
            weights = jnp.where(lane == k, pattern_ref[t, i * blocks + k].astype(jnp.float32), weights)
        pieces.append(trans_ref[0, i * block:(i + 1) * block, :] * weights)
    dense = jnp.concatenate(pieces, axis=0)
    dense_ref[0] = dense
    fgain, sgain = fgain_ref[...], sgain_ref[...]
    gain = fgain * obs_ref[0, pl.ds(t, 1), :].astype(jnp.float32)
    keep = 1.0 - gain
    drive = gain * meas_ref[0, pl.ds(t, 1), :]
    gain_ref[j, pl.ds(c, 1), :] = gain
    drive_ref[j, pl.ds(c, 1), :] = drive

    @pl.when(j == 0)
    def _():
        turned = dense.T
        state[c, 0:width, :] = turned * keep
        state[c, width:2 * width, :] = turned * sgain
        state[c, 2 * width:, :] = jnp.broadcast_to(drive, (2 * SUB, width))

    @pl.when(j > 0)
    def _():
        rows = lax.broadcasted_iota(jnp.int32, (width, width), 0)
        cols = lax.broadcasted_iota(jnp.int32, (width, width), 1)
        on_diagonal = rows == cols
        diagonal = jnp.sum(jnp.where(on_diagonal, dense, 0.0), axis=0, keepdims=True)
        rest_high, rest_low = split(jnp.where(on_diagonal, 0.0, dense))
        now = state[c]
        high, low = split(now)
        new = now * diagonal + (
            dot_rhs_t(high, rest_high) + (dot_rhs_t(low, rest_high) + dot_rhs_t(high, rest_low))
        )
        state[c, 0:width, :] = new[0:width] * keep
        state[c, width:2 * width, :] = new[width:2 * width] * sgain
        state[c, 2 * width:, :] = new[2 * width:] * keep + drive

    @pl.when(j == length - 1)
    def _():
        pmap_ref[0] = state[c, width:2 * width, :]

        @pl.when(c == 0)
        def _():
            pre[...] = state[0]

        @pl.when(c > 0)
        def _():
            shift = state[c, 2 * width:, :]
            pre[0:width, :] = jnp.dot(pre[0:width, :], state[c, 0:width, :], precision=HIGHEST)
            pre[2 * width:, :] = jnp.dot(pre[2 * width:, :], state[c, 0:width, :], precision=HIGHEST) + shift
            pre[width:2 * width, :] = jnp.dot(
                pre[width:2 * width, :], state[c, width:2 * width, :], precision=HIGHEST)

        apre_ref[0] = pre[0:width, :]
        bpre_ref[0] = pre[2 * width:2 * width + SUB, :]

        @pl.when(c == chunks - 1)
        def _():
            ptot_ref[...] = pre[width:2 * width, :]


def chain(transitions, pattern, obs, meas, fgain, sgain):
    steps, width, _ = transitions.shape
    length = steps // CHUNKS
    at_end = lambda j, c, *_: (c * (j // (length - 1)), 0, 0)
    fixed = lambda j, c, *_: (0, 0)
    f32 = jnp.float32
    return pl.pallas_call(
        chain_kernel,
        grid_spec=pltpu.PrefetchScalarGridSpec(
            num_scalar_prefetch=1,
            grid=(length, CHUNKS),
            in_specs=[
                pl.BlockSpec((1, width, width), lambda j, c, *_: (c * length + j, 0, 0)),
                pl.BlockSpec((1, steps, width), lambda j, c, *_: (0, 0, 0)),
                pl.BlockSpec((1, steps, width), lambda j, c, *_: (0, 0, 0)),
                pl.BlockSpec((1, width), fixed),
                pl.BlockSpec((1, width), fixed),
            ],
            out_specs=[
                pl.BlockSpec((1, width, width), lambda j, c, *_: (c * length + j, 0, 0)),
                pl.BlockSpec((1, width, width), at_end),
                pl.BlockSpec((1, SUB, width), at_end),
                pl.BlockSpec((1, width, width), at_end),
                pl.BlockSpec((width, width), fixed),
                pl.BlockSpec((length, CHUNKS, width), lambda *_: (0, 0, 0)),
                pl.BlockSpec((length, CHUNKS, width), lambda *_: (0, 0, 0)),
            ],
            scratch_shapes=[
                pltpu.VMEM((CHUNKS, 2 * width + 2 * SUB, width), f32),
                pltpu.VMEM((2 * width + 2 * SUB, width), f32),
            ],
        ),
        out_shape=[
            jax.ShapeDtypeStruct((steps, width, width), f32),
            jax.ShapeDtypeStruct((CHUNKS, width, width), f32),
            jax.ShapeDtypeStruct((CHUNKS, SUB, width), f32),
            jax.ShapeDtypeStruct((CHUNKS, width, width), f32),
            jax.ShapeDtypeStruct((width, width), f32),
            jax.ShapeDtypeStruct((length, CHUNKS, width), f32),
            jax.ShapeDtypeStruct((length, CHUNKS, width), f32),
        ],
        compiler_params=pltpu.CompilerParams(vmem_limit_bytes=VMEM_BYTES),
    )(pattern, transitions, obs, meas, fgain, sgain)


def relay_kernel(count, reverse, map_ref, shift_ref, first_ref, out_ref, inbox, outbox, send_sem, recv_sem):
    me = lax.axis_index("tm")
    place = count - 1 - me if reverse else me
    step = -1 if reverse else 1
    barrier = pltpu.get_barrier_semaphore()

    @pl.when(place > 0)
    def _():
        pl.semaphore_signal(barrier, inc=1, device_id={"tm": me - step})

    @pl.when(place < count - 1)
    def _():
        pl.semaphore_signal(barrier, inc=1, device_id={"tm": me + step})

    ends = (place == 0) | (place == count - 1)

    @pl.when(ends)
    def _():
        pl.semaphore_wait(barrier, 1)

    @pl.when(jnp.logical_not(ends))
    def _():
        pl.semaphore_wait(barrier, 2)

    arrow = functools.partial(
        pltpu.make_async_remote_copy, src_ref=outbox, dst_ref=inbox, send_sem=send_sem, recv_sem=recv_sem)

    @pl.when(place > 0)
    def _():
        arrow(device_id={"tm": me - step}).wait_recv()
        out_ref[...] = inbox[...]

    @pl.when(place == 0)
    def _():
        out_ref[...] = first_ref[...]

    @pl.when(place < count - 1)
    def _():
        entering = out_ref[...]
        if reverse:
            moved = jnp.sum(map_ref[...] * entering[0:1], axis=1, keepdims=True)
            row = jnp.broadcast_to(moved, (moved.shape[0], LANES)).T[0:SUB]
        else:
            column = to_column(entering)[:, 0:1]
            row = jnp.broadcast_to(
                jnp.sum(map_ref[...] * column, axis=0, keepdims=True), entering.shape)
        outbox[...] = row + shift_ref[...]
        going = arrow(device_id={"tm": me + step})
        going.start()
        going.wait_send()


def relay(maps, shift, first, reverse, ident):
    count = lax.axis_size("tm")
    width = first.shape[1]
    whole = pl.BlockSpec((SUB, width), lambda i: (0, 0))
    last = maps.shape[0] - 1 if maps.ndim == 3 else 0
    map_spec = (pl.BlockSpec((None, width, width), lambda i: (last, 0, 0)) if maps.ndim == 3
                else pl.BlockSpec((width, width), lambda i: (0, 0)))
    shift_spec = (pl.BlockSpec((None, SUB, width), lambda i: (last, 0, 0)) if shift.ndim == 3 else whole)
    return pl.pallas_call(
        functools.partial(relay_kernel, count, reverse),
        grid=(1,),
        in_specs=[map_spec, shift_spec, whole],
        out_specs=whole,
        out_shape=jax.ShapeDtypeStruct((SUB, width), jnp.float32),
        scratch_shapes=[
            pltpu.VMEM((SUB, width), jnp.float32),
            pltpu.VMEM((SUB, width), jnp.float32),
            pltpu.SemaphoreType.DMA,
            pltpu.SemaphoreType.DMA,
        ],
        compiler_params=pltpu.CompilerParams(collective_id=ident, has_side_effects=True),
    )(maps, shift, first)


def turned_step(dense_ref, j, values):
    columns = to_column(values)
    rows = [
        jnp.sum(dense_ref[c, j] * columns[:, c:c + 1], axis=0, keepdims=True) for c in range(CHUNKS)
    ]
    return jnp.concatenate(rows, axis=0)


def filter_kernel(dense_ref, apre_ref, bpre_ref, pmap_ref, start_ref, gain_ref, drive_ref, sgain_ref,
                  filtered_ref, change_ref, carried_ref, shift_ref):
    chunks, length, width, _ = dense_ref.shape
    column = to_column(start_ref[...])[:, 0:1]
    rows = [start_ref[0:1, :]]
    for c in range(chunks - 1):
        rows.append(bpre_ref[c, 0:1, :] + jnp.sum(apre_ref[c] * column, axis=0, keepdims=True))
    start = jnp.concatenate(rows, axis=0)
    lane = lax.broadcasted_iota(jnp.int32, (width, LANES), 1)

    def forward(j, state):
        gathered = jnp.zeros((width, LANES), jnp.float32)
        for c in range(chunks):
            moved = jnp.sum(dense_ref[c, j] * state[c:c + 1, :], axis=1, keepdims=True)
            gathered = jnp.where(lane == c, moved, gathered)
        predict = gathered.T[0:chunks]
        new = (1.0 - gain_ref[j]) * predict + drive_ref[j]
        filtered_ref[j] = new
        change_ref[j] = new - predict
        return new

    lax.fori_loop(0, length, forward, start)

    def backward(i, carried):
        j = length - 1 - i
        return turned_step(dense_ref, j, change_ref[j] + sgain_ref[...] * carried)

    carried = lax.fori_loop(0, length, backward, jnp.zeros((chunks, width), jnp.float32))
    carried_ref[...] = carried
    total = carried[chunks - 1:chunks]
    for c in range(chunks - 2, -1, -1):
        moved = jnp.sum(pmap_ref[c] * total, axis=1, keepdims=True)
        total = carried[c:c + 1] + jnp.broadcast_to(moved, (width, LANES)).T[0:1]
    shift_ref[...] = jnp.broadcast_to(total, (SUB, width))


def smoother_kernel(dense_ref, pmap_ref, enter_ref, carried_ref, filtered_ref, change_ref, sgain_ref,
                    smoothed_ref, info_ref, residuals):
    chunks, length, width, _ = dense_ref.shape
    carried = carried_ref[...]
    rows = [enter_ref[0:1, :]]
    for c in range(chunks - 1, 0, -1):
        moved = jnp.sum(pmap_ref[c] * rows[0], axis=1, keepdims=True)
        rows.insert(0, carried[c:c + 1] + jnp.broadcast_to(moved, (width, LANES)).T[0:1])
    start = jnp.concatenate(rows, axis=0)

    def backward(i, carry):
        j = length - 1 - i
        lifted = sgain_ref[...] * carry
        smoothed = filtered_ref[j] + lifted
        for c in range(chunks):
            smoothed_ref[0, pl.ds(c * length + j, 1), :] = smoothed[c:c + 1]
        residual = change_ref[j] + lifted
        residuals[j] = residual
        return turned_step(dense_ref, j, residual)

    lax.fori_loop(0, length, backward, start)
    every = residuals[...].reshape(length * chunks, width)
    info_ref[...] = lax.dot_general(
        every, every, (((0,), (0,)), ((), ())), precision=HIGHEST, preferred_element_type=jnp.float32)


def shards(transitions, pattern, obs_mask, measured, prior_mean, filter_gain, smooth_gain):
    steps, width, _ = transitions.shape
    length = steps // CHUNKS
    f32 = jnp.float32
    fgain, sgain = filter_gain[None, :], smooth_gain[None, :]
    dense, apre, bpre, pmap, ptot, gain, drive = chain(
        transitions, pattern.reshape(steps, -1), obs_mask, measured, fgain, sgain)
    dense = dense.reshape(CHUNKS, length, width, width)
    first = jnp.broadcast_to(prior_mean, (SUB, width))
    start = relay(apre, bpre, first, False, 0)
    per_step = jax.ShapeDtypeStruct((length, CHUNKS, width), f32)
    row = jax.ShapeDtypeStruct((SUB, width), f32)
    params = pltpu.CompilerParams(vmem_limit_bytes=VMEM_BYTES)
    vmem = pl.BlockSpec(memory_space=pltpu.VMEM)
    filtered, change, carried, shift = pl.pallas_call(
        filter_kernel,
        in_specs=[vmem] * 8,
        out_specs=[vmem] * 4,
        out_shape=[per_step, per_step, row, row],
        compiler_params=params,
    )(dense, apre, bpre, pmap, start, gain, drive, sgain)
    entering = relay(ptot, shift, jnp.zeros((SUB, width), f32), True, 1)
    smoothed, local_info = pl.pallas_call(
        smoother_kernel,
        in_specs=[vmem] * 7,
        out_specs=[vmem] * 2,
        out_shape=[jax.ShapeDtypeStruct((1, steps, width), f32), jax.ShapeDtypeStruct((width, width), f32)],
        scratch_shapes=[pltpu.VMEM((length, CHUNKS, width), f32)],
        compiler_params=params,
    )(dense, pmap, entering, carried, filtered, change, sgain)
    total_info = lax.psum(local_info, ("tm", "exp"))
    information = total_info / (steps * lax.axis_size("tm") * lax.axis_size("exp"))
    return smoothed, information


def solution(mesh):
    in_specs = (
        P("tm", None, None),
        P("tm", None, None),
        P("exp", "tm", None),
        P("exp", "tm", None),
        P("exp", None),
        P(),
        P(),
    )
    out_specs = (P("exp", "tm", None), P())
    return jax.shard_map(shards, mesh=mesh, in_specs=in_specs, out_specs=out_specs, check_vma=False)
```

time: 676 us -> 275 us (0.41); the launches traced: 666 us -> 274 us
  matrix products: 383 us -> 0 us
  Pallas kernels: 0 us -> 133 us
  local copies, waits for them, and re-layouts: 63 us -> 2.59 us
  blocking collectives: 38.6 us -> 0 us
  other arithmetic: 33 us -> 1.67 us
  loops' own time: 9.82 us -> 0 us
    dot_general x294 -> x0, matrix products: 383 us -> none  [the longest x128 157 us: update(): predict = jnp.dot(trans_step, state, precision=lax.Precision.HIGHEST)]
    pallas_call x0 -> x5, Pallas kernels: none -> 133 us  [the longest x1 54.7 us: chain(): pl.pallas_call(chain_kernel, grid_spec=pltpu.PrefetchScalarGridSpec(num_s...]
    mul x2 -> x0, local copies, waits for them, and re-layouts: 41.7 us -> none  [masked_dense(): return (reshaped * weights).reshape(count_steps, state_width, state_width)]
    all_gather x2 -> x0, blocking collectives: 38.6 us -> none  [entering(): everything = jax.tree.map(lambda part: lax.all_gather(part, axis), x)]
    mul x3 -> x0, other arithmetic: 25 us -> none  [the longest x1 17.7 us: shards(): filter_map = chain_product(keep_rows[:, :, None] * dense_steps)]
    dynamic_update_slice x256 -> x0, local copies, waits for them, and re-layouts: 12.1 us -> none  [run_filter(): lax.scan(update, start_state, (dense_steps, keep_rows, drive_terms))]
    another operation x6 -> x0, loops' own time: 9.82 us -> none  [the longest x2 5.2 us: run_filter(): lax.scan(update, start_state, (dense_steps, keep_rows, drive_terms))]
    dynamic_slice x272 -> x0, local copies, waits for them, and re-layouts: 8.83 us -> none  [the longest x256 7.86 us: run_filter(): lax.scan(update, start_state, (dense_steps, keep_rows, drive_terms))]
  transfers between devices with their start and end apart: 3 -> 1, of which waited for: 1 -> 1; matrix products, arithmetic and copies ran while one was open for 45% -> 0% of each run, Pallas kernels for 0% -> 0%
where the time goes in v1:
time: 275 us; the launch traced here: 274 us
  Pallas kernels  133 us (48%)
  waiting for transfers between devices  122 us (44%)
  between operations  14.1 us (5%)
    psum x1, waiting for transfers between devices, shards(): total_info = lax.psum(local_info, ('tm', 'exp'))  122 us
    pallas_call x1, Pallas kernels, chain(): pl.pallas_call(chain_kernel, grid_spec=pltpu.PrefetchScalarGridSpec(num_s...  54.7 us
    pallas_call x2, Pallas kernels, relay(): pl.pallas_call(functools.partial(relay_kernel, count, reverse), grid=(1,)...  48.7 us
    pallas_call x1, Pallas kernels, shards(): pl.pallas_call(filter_kernel, in_specs=[vmem] * 8, out_specs=[vmem] * 4,...  16.6 us
    pallas_call x1, Pallas kernels, shards(): pl.pallas_call(smoother_kernel, in_specs=[vmem] * 7, out_specs=[vmem] * 2...  13 us
  transfers between devices with their start and end apart: 1, of which 1 were waited for; matrix products, arithmetic and copies ran while one was open for 0% of the time, Pallas kernels for 0%

profile of v1, /device:TPU:0, one launch (start us, length us, event | category | flops | bytes accessed | tf_op | source)
XLA Modules:
  0.0 273.7 jit_solution(12132340314986710547)
XLA Ops:
  7.2 0.0 copy-start
  7.2 0.0 all-reduce.2.cloned.1.call-start
  7.2 1.4 copy.10.pattern_ref
  8.6 54.7 %shard_map.86 = (f32[64,256,256]{2,1,0:T(8,128)}, f32[8,256,256]{2,1,0:T(8,128)}, f32[8,8,256]{2,1,0:T(8,128)}, f32[8,256,256]{2,1,0:T(8,128)}, f32[256,256]{1,0...) custom-call(s32[64,16]{1,0:T(8,128)} %copy.10.pattern_ref, f32[64,256,256]{2,1,0:T(8,128)} %trans_ref.1, ...), custom_call_target="tpu_custom_call" | custom-call | tf_op jit(solution)/shard_map/pallas_call | solution.py:110
  63.3 0.0 copy-done
  63.3 0.6 broadcast_in_dim.19.first_ref
  63.9 6.1 %shard_map.87.start_ref = f32[8,256]{1,0:T(8,128)} custom-call(f32[8,256,256]{2,1,0:T(8,128)} %get-tuple-element.18.map_ref.apre_ref, f32[8,8,256]{2,1,0:T(8,128)} %get-tuple-element.19.shift_ref.bpre_ref, f32[8,256]{1,0:T(8,128)} %broadcast_in_dim.19.first_ref), custom_call_target="tpu_custom_call" | custom-call | tf_op jit(solution)/shard_map/pallas_call | solution.py:209
  70.0 16.6 %shard_map.88 = (f32[8,8,256]{2,1,0:T(8,128)}, f32[8,8,256]{2,1,0:T(8,128)}, f32[8,256]{1,0:T(8,128)}, f32[8,256]{1,0:T(8,128)}) custom-call(f32[8,8,256,256]{3,2,1,0:T(8,128)} %bitcast.5, f32[8,256,256]{2,1,0:T(8,128)} %get-tuple-element.18.map_ref.apre_ref, f32[8,8,256]{2,1,0:T(8,128)} %get-tuple-element.19.shift_ref.bpre_ref, ...), custom_call_target="tpu_custom_call" | custom-call | tf_op jit(solution)/shard_map/pallas_call | solution.py:309
  86.6 0.6 broadcast_in_dim.20.first_ref
  87.2 42.5 %shard_map.89.enter_ref = f32[8,256]{1,0:T(8,128)} custom-call(f32[256,256]{1,0:T(8,128)} %get-tuple-element.17.map_ref, f32[8,256]{1,0:T(8,128)} %get-tuple-element.22.shift_ref, f32[8,256]{1,0:T(8,128)} %broadcast_in_dim.20.first_ref), custom_call_target="tpu_custom_call" | custom-call | tf_op jit(solution)/shard_map/pallas_call | solution.py:209
  129.7 13.0 %shard_map.90 = (f32[1,64,256]{2,1,0:T(8,128)}, f32[256,256]{1,0:T(8,128)}) custom-call(f32[8,8,256,256]{3,2,1,0:T(8,128)} %bitcast.6, f32[8,256,256]{2,1,0:T(8,128)} %get-tuple-element.16.pmap_ref, f32[8,256]{1,0:T(8,128)} %shard_map.89.enter_ref, f32[8,256]{1,0:T(8,128)} %get-tuple-element.23.carried_ref, f32[8,8,256]{2,1,0:T(8,128)} %get-tuple-element.24.filtered_ref, ...), custom_call_target="tpu_custom_call" | custom-call | tf_op jit(solution)/shard_map/pallas_call | solution.py:317
  142.8 0.0 all-reduce.2.cloned.1.call-update
  142.8 122.4 %all-reduce.2.cloned.1.call-done = f32[256,256]{1,0:T(8,128)} async-done(((f32[256,256]{1,0:T(8,128)}), f32[256,256]{1,0:T(8,128)}) %all-reduce.2.cloned.1.call-update) | async-done | bytes 262160 | tf_op jit(solution)/shard_map/psum | solution.py:325
  265.2 1.7 broadcast_multiply_fusion
Async XLA Ops:
  7.2 56.1 %copy-start = (f32[1,256]{1,0:T(1,128)S(1)}, f32[1,256]{1,0:T(1,128)}, u32[]{:S(2)}) copy-start(f32[1,256]{1,0:T(1,128)} %param.11) | copy-start | bytes 3076
  7.2 258.0 %all-reduce.2.cloned.1.call-start = ((), (), s32[]{:S(2)}) async-start(), calls=%async_computation | async-start | bytes 524288 | tf_op jit(solution)/shard_map/psum | solution.py:325
Sparse Core Ops, SparseCore 0:
  142.9 122.2 all-reduce.1

commit v2 on v1

--- a/solution.py
+++ b/solution.py
@@ -222,74 +222,164 @@
     )(maps, shift, first)
 
 
-def turned_step(dense_ref, j, values):
+def turned_step(dense_ref, values):
     columns = to_column(values)
     rows = [
-        jnp.sum(dense_ref[c, j] * columns[:, c:c + 1], axis=0, keepdims=True) for c in range(CHUNKS)
+        jnp.sum(dense_ref[c] * columns[:, c:c + 1], axis=0, keepdims=True) for c in range(CHUNKS)
     ]
     return jnp.concatenate(rows, axis=0)
 
 
 def filter_kernel(dense_ref, apre_ref, bpre_ref, pmap_ref, start_ref, gain_ref, drive_ref, sgain_ref,
-                  filtered_ref, change_ref, carried_ref, shift_ref):
-    chunks, length, width, _ = dense_ref.shape
-    column = to_column(start_ref[...])[:, 0:1]
-    rows = [start_ref[0:1, :]]
-    for c in range(chunks - 1):
-        rows.append(bpre_ref[c, 0:1, :] + jnp.sum(apre_ref[c] * column, axis=0, keepdims=True))
-    start = jnp.concatenate(rows, axis=0)
-    lane = lax.broadcasted_iota(jnp.int32, (width, LANES), 1)
-
-    def forward(j, state):
+                  filtered_ref, change_ref, carried_ref, shift_ref, state):
+    i, length = pl.program_id(0), filtered_ref.shape[0]
+    chunks, width, _ = dense_ref.shape
+
+    @pl.when(i == 0)
+    def _():
+        column = to_column(start_ref[...])[:, 0:1]
+        rows = [start_ref[0:1, :]]
+        for c in range(chunks - 1):
+            rows.append(bpre_ref[c, 0:1, :] + jnp.sum(apre_ref[c] * column, axis=0, keepdims=True))
+        state[...] = jnp.concatenate(rows, axis=0)
+
+    @pl.when(i < length)
+    def _():
+        lane = lax.broadcasted_iota(jnp.int32, (width, LANES), 1)
         gathered = jnp.zeros((width, LANES), jnp.float32)
         for c in range(chunks):
-            moved = jnp.sum(dense_ref[c, j] * state[c:c + 1, :], axis=1, keepdims=True)
+            moved = jnp.sum(dense_ref[c] * state[c:c + 1, :], axis=1, keepdims=True)
             gathered = jnp.where(lane == c, moved, gathered)
         predict = gathered.T[0:chunks]
-        new = (1.0 - gain_ref[j]) * predict + drive_ref[j]
-        filtered_ref[j] = new
-        change_ref[j] = new - predict
-        return new
-
-    lax.fori_loop(0, length, forward, start)
-
-    def backward(i, carried):
-        j = length - 1 - i
-        return turned_step(dense_ref, j, change_ref[j] + sgain_ref[...] * carried)
-
-    carried = lax.fori_loop(0, length, backward, jnp.zeros((chunks, width), jnp.float32))
-    carried_ref[...] = carried
-    total = carried[chunks - 1:chunks]
-    for c in range(chunks - 2, -1, -1):
-        moved = jnp.sum(pmap_ref[c] * total, axis=1, keepdims=True)
-        total = carried[c:c + 1] + jnp.broadcast_to(moved, (width, LANES)).T[0:1]
-    shift_ref[...] = jnp.broadcast_to(total, (SUB, width))
+        new = (1.0 - gain_ref[i]) * predict + drive_ref[i]
+        filtered_ref[i] = new
+        change_ref[i] = new - predict
+        state[...] = new
+
+    @pl.when(i == length)
+    def _():
+        state[...] = jnp.zeros_like(state)
+
+    @pl.when(i >= length)
+    def _():
+        j = 2 * length - 1 - i
+        state[...] = turned_step(dense_ref, change_ref[j] + sgain_ref[...] * state[...])
+
+    @pl.when(i == 2 * length - 1)
+    def _():
+        carried = state[...]
+        carried_ref[...] = carried
+        total = carried[chunks - 1:chunks]
+        for c in range(chunks - 2, -1, -1):
+            moved = jnp.sum(pmap_ref[c] * total, axis=1, keepdims=True)
+            total = carried[c:c + 1] + jnp.broadcast_to(moved, (width, LANES)).T[0:1]
+        shift_ref[...] = jnp.broadcast_to(total, (SUB, width))
 
 
 def smoother_kernel(dense_ref, pmap_ref, enter_ref, carried_ref, filtered_ref, change_ref, sgain_ref,
-                    smoothed_ref, info_ref, residuals):
-    chunks, length, width, _ = dense_ref.shape
-    carried = carried_ref[...]
-    rows = [enter_ref[0:1, :]]
-    for c in range(chunks - 1, 0, -1):
-        moved = jnp.sum(pmap_ref[c] * rows[0], axis=1, keepdims=True)
-        rows.insert(0, carried[c:c + 1] + jnp.broadcast_to(moved, (width, LANES)).T[0:1])
-    start = jnp.concatenate(rows, axis=0)
-
-    def backward(i, carry):
-        j = length - 1 - i
-        lifted = sgain_ref[...] * carry
-        smoothed = filtered_ref[j] + lifted
-        for c in range(chunks):
-            smoothed_ref[0, pl.ds(c * length + j, 1), :] = smoothed[c:c + 1]
-        residual = change_ref[j] + lifted
-        residuals[j] = residual
-        return turned_step(dense_ref, j, residual)
-
-    lax.fori_loop(0, length, backward, start)
-    every = residuals[...].reshape(length * chunks, width)
-    info_ref[...] = lax.dot_general(
-        every, every, (((0,), (0,)), ((), ())), precision=HIGHEST, preferred_element_type=jnp.float32)
+                    smoothed_ref, info_ref, residuals, state):
+    i, length = pl.program_id(0), filtered_ref.shape[0]
+    chunks, width, _ = dense_ref.shape
+
+    @pl.when(i == 0)
+    def _():
+        carried = carried_ref[...]
+        rows = [enter_ref[0:1, :]]
+        for c in range(chunks - 1, 0, -1):
+            moved = jnp.sum(pmap_ref[c] * rows[0], axis=1, keepdims=True)
+            rows.insert(0, carried[c:c + 1] + jnp.broadcast_to(moved, (width, LANES)).T[0:1])
+        state[...] = jnp.concatenate(rows, axis=0)
+
+    j = length - 1 - i
+    lifted = sgain_ref[...] * state[...]
+    smoothed = filtered_ref[j] + lifted
+    for c in range(chunks):
+        smoothed_ref[0, pl.ds(c * length + j, 1), :] = smoothed[c:c + 1]
+    residual = change_ref[j] + lifted
+    residuals[j] = residual
+
+    @pl.when(i < length - 1)
+    def _():
+        state[...] = turned_step(dense_ref, residual)
+
+    @pl.when(i == length - 1)
+    def _():
+        every = residuals[...].reshape(length * chunks, width)
+        info_ref[...] = lax.dot_general(
+            every, every, (((0,), (0,)), ((), ())), precision=HIGHEST, preferred_element_type=jnp.float32)
+
+
+def total_kernel(parts, blocks, scale, local_ref, out_ref, part, box_e, box_t, send_sem, recv_sem):
+    e, t = lax.axis_index("exp"), lax.axis_index("tm")
+    barrier = pltpu.get_barrier_semaphore()
+    e_peers = [lax.rem(e + k, parts) for k in range(1, parts)]
+    t_peers = [lax.rem(t + k, blocks) for k in range(1, blocks)]
+    for peer in e_peers:
+        pl.semaphore_signal(barrier, inc=1, device_id={"exp": peer})
+    for peer in t_peers:
+        pl.semaphore_signal(barrier, inc=1, device_id={"tm": peer})
+    pl.semaphore_wait(barrier, parts + blocks - 2)
+
+    def send(src, dst, number, device):
+        copy = pltpu.make_async_remote_copy(
+            src_ref=src, dst_ref=dst, send_sem=send_sem.at[number], recv_sem=recv_sem.at[number],
+            device_id=device)
+        copy.start()
+        return copy
+
+    first = [send(local_ref.at[p], box_e.at[k], k, {"exp": p}) for k, p in enumerate(e_peers)]
+    base = len(first)
+    value = local_ref[e]
+    for k, copy in enumerate(first):
+        copy.wait_recv()
+        value = value + box_e[k]
+    part[...] = value
+    second = [send(part.at[p], box_t.at[k], base + k, {"tm": p}) for k, p in enumerate(t_peers)]
+    base += len(second)
+    mine = part[t]
+    for k, copy in enumerate(second):
+        copy.wait_recv()
+        mine = mine + box_t[k]
+    out_ref[e, t] = mine * scale
+    third = [send(out_ref.at[e, t], out_ref.at[e, t], base + k, {"tm": p}) for k, p in enumerate(t_peers)]
+    base += len(third)
+    for k, copy in enumerate(third):
+        sender = lax.rem(t + blocks - 1 - k, blocks)
+        pltpu.make_async_remote_copy(
+            src_ref=out_ref.at[e, sender], dst_ref=out_ref.at[e, sender], send_sem=send_sem.at[base - len(third) + k],
+            recv_sem=recv_sem.at[base - len(third) + k], device_id={"tm": sender}).wait_recv()
+    fourth = [send(out_ref.at[e], out_ref.at[e], base + k, {"exp": p}) for k, p in enumerate(e_peers)]
+    for k, copy in enumerate(fourth):
+        sender = lax.rem(e + parts - 1 - k, parts)
+        pltpu.make_async_remote_copy(
+            src_ref=out_ref.at[sender], dst_ref=out_ref.at[sender], send_sem=send_sem.at[base + k],
+            recv_sem=recv_sem.at[base + k], device_id={"exp": sender}).wait_recv()
+    for copy in first + second + third + fourth:
+        copy.wait_send()
+
+
+def total(local, scale, ident):
+    parts, blocks = lax.axis_size("exp"), lax.axis_size("tm")
+    width = local.shape[0]
+    rows = width // (parts * blocks)
+    copies = 2 * (parts - 1) + 2 * (blocks - 1)
+    f32 = jnp.float32
+    vmem = pl.BlockSpec(memory_space=pltpu.VMEM)
+    summed = pl.pallas_call(
+        functools.partial(total_kernel, parts, blocks, scale),
+        in_specs=[vmem],
+        out_specs=vmem,
+        out_shape=jax.ShapeDtypeStruct((parts, blocks, rows, width), f32),
+        scratch_shapes=[
+            pltpu.VMEM((blocks, rows, width), f32),
+            pltpu.VMEM((parts - 1, blocks, rows, width), f32),
+            pltpu.VMEM((blocks - 1, rows, width), f32),
+            pltpu.SemaphoreType.DMA((copies,)),
+            pltpu.SemaphoreType.DMA((copies,)),
+        ],
+        compiler_params=pltpu.CompilerParams(collective_id=ident, has_side_effects=True),
+    )(local.reshape(parts, blocks, rows, width))
+    return summed.reshape(width, width)
 
 
 def shards(transitions, pattern, obs_mask, measured, prior_mean, filter_gain, smooth_gain):
@@ -305,25 +395,32 @@
     per_step = jax.ShapeDtypeStruct((length, CHUNKS, width), f32)
     row = jax.ShapeDtypeStruct((SUB, width), f32)
     params = pltpu.CompilerParams(vmem_limit_bytes=VMEM_BYTES)
-    vmem = pl.BlockSpec(memory_space=pltpu.VMEM)
+    fixed = lambda array: pl.BlockSpec(array.shape, lambda i: (0,) * len(array.shape))
+    moving = lambda at: pl.BlockSpec((CHUNKS, None, width, width), lambda i: (0, at(i), 0, 0))
+    others = (apre, bpre, pmap, start, gain, drive, sgain)
     filtered, change, carried, shift = pl.pallas_call(
         filter_kernel,
-        in_specs=[vmem] * 8,
-        out_specs=[vmem] * 4,
+        grid=(2 * length,),
+        in_specs=[moving(lambda i: jnp.minimum(i, 2 * length - 1 - i))] + [fixed(x) for x in others],
+        out_specs=[fixed(x) for x in (per_step, per_step, row, row)],
         out_shape=[per_step, per_step, row, row],
+        scratch_shapes=[pltpu.VMEM((CHUNKS, width), f32)],
         compiler_params=params,
-    )(dense, apre, bpre, pmap, start, gain, drive, sgain)
+    )(dense, *others)
     entering = relay(ptot, shift, jnp.zeros((SUB, width), f32), True, 1)
+    others = (pmap, entering, carried, filtered, change, sgain)
+    outs = [jax.ShapeDtypeStruct((1, steps, width), f32), jax.ShapeDtypeStruct((width, width), f32)]
     smoothed, local_info = pl.pallas_call(
         smoother_kernel,
-        in_specs=[vmem] * 7,
-        out_specs=[vmem] * 2,
-        out_shape=[jax.ShapeDtypeStruct((1, steps, width), f32), jax.ShapeDtypeStruct((width, width), f32)],
-        scratch_shapes=[pltpu.VMEM((length, CHUNKS, width), f32)],
+        grid=(length,),
+        in_specs=[moving(lambda i: length - 1 - i)] + [fixed(x) for x in others],
+        out_specs=[fixed(x) for x in outs],
+        out_shape=outs,
+        scratch_shapes=[pltpu.VMEM((length, CHUNKS, width), f32), pltpu.VMEM((CHUNKS, width), f32)],
         compiler_params=params,
-    )(dense, pmap, entering, carried, filtered, change, sgain)
-    total_info = lax.psum(local_info, ("tm", "exp"))
-    information = total_info / (steps * lax.axis_size("tm") * lax.axis_size("exp"))
+    )(dense, *others)
+    scale = 1.0 / (steps * lax.axis_size("tm") * lax.axis_size("exp"))
+    information = total(local_info, scale, 2)
     return smoothed, information
 
 

time: 275 us -> 163 us (0.59)
  waiting for transfers between devices: 122 us -> 0 us
  Pallas kernels: 133 us -> 157 us
  between operations: 14.1 us -> 0.67 us
    psum x1 -> x0, waiting for transfers between devices: 122 us -> none  [shards(): total_info = lax.psum(local_info, ('tm', 'exp'))]
    pallas_call x2 -> x3, Pallas kernels: 29.6 us -> 53.2 us  [the longest x1 21.4 us: shards(): pl.pallas_call(filter_kernel, grid=(2 * length,), in_specs=[moving(lambda...]
  transfers between devices with their start and end apart: 1 -> 0, of which waited for: 1 -> 0; matrix products, arithmetic and copies ran while one was open for 0% -> 0% of each run, Pallas kernels for 0% -> 0%
where the time goes in v2:
time: 163 us; the launch traced here: 161 us
  Pallas kernels  157 us (96%)
  local copies, waits for them, and re-layouts  4.25 us (3%)
    pallas_call x1, Pallas kernels, chain(): pl.pallas_call(chain_kernel, grid_spec=pltpu.PrefetchScalarGridSpec(num_s...  54.6 us
    pallas_call x2, Pallas kernels, relay(): pl.pallas_call(functools.partial(relay_kernel, count, reverse), grid=(1,)...  48.7 us
    pallas_call x1, Pallas kernels, shards(): pl.pallas_call(filter_kernel, grid=(2 * length,), in_specs=[moving(lambda...  21.4 us
    pallas_call x1, Pallas kernels, total(): pl.pallas_call(functools.partial(total_kernel, parts, blocks, scale), in_...  19.6 us
    pallas_call x1, Pallas kernels, shards(): pl.pallas_call(smoother_kernel, grid=(length,), in_specs=[moving(lambda i...  12.2 us

profile of v2, /device:TPU:0, one launch (start us, length us, event | category | flops | bytes accessed | tf_op | source)
XLA Modules:
  0.0 161.4 jit_solution(13404378950783995790)
XLA Ops:
  0.6 0.0 copy-start
  0.6 1.4 copy.10.pattern_ref
  2.0 54.6 %shard_map.86 = (f32[64,256,256]{2,1,0:T(8,128)}, f32[8,256,256]{2,1,0:T(8,128)}, f32[8,8,256]{2,1,0:T(8,128)}, f32[8,256,256]{2,1,0:T(8,128)}, f32[256,256]{1,0...) custom-call(s32[64,16]{1,0:T(8,128)} %copy.10.pattern_ref, f32[64,256,256]{2,1,0:T(8,128)} %trans_ref.1, ...), custom_call_target="tpu_custom_call" | custom-call | tf_op jit(solution)/shard_map/pallas_call | solution.py:110
  56.7 0.0 copy-done
  56.7 0.6 broadcast_in_dim.19.first_ref
  57.3 6.1 %shard_map.87.start_ref = f32[8,256]{1,0:T(8,128)} custom-call(f32[8,256,256]{2,1,0:T(8,128)} %get-tuple-element.18.map_ref.apre_ref, f32[8,8,256]{2,1,0:T(8,128)} %get-tuple-element.19.shift_ref.bpre_ref, f32[8,256]{1,0:T(8,128)} %broadcast_in_dim.19.first_ref), custom_call_target="tpu_custom_call" | custom-call | tf_op jit(solution)/shard_map/pallas_call | solution.py:209
  63.4 21.4 %shard_map.88 = (f32[8,8,256]{2,1,0:T(8,128)}, f32[8,8,256]{2,1,0:T(8,128)}, f32[8,256]{1,0:T(8,128)}, f32[8,256]{1,0:T(8,128)}) custom-call(f32[8,8,256,256]{3,2,1,0:T(8,128)} %bitcast.7, f32[8,256,256]{2,1,0:T(8,128)} %get-tuple-element.18.map_ref.apre_ref, f32[8,8,256]{2,1,0:T(8,128)} %get-tuple-element.19.shift_ref.bpre_ref, ...), custom_call_target="tpu_custom_call" | custom-call | tf_op jit(solution)/shard_map/pallas_call | solution.py:401
  84.9 0.6 broadcast_in_dim.20.first_ref
  85.5 42.5 %shard_map.89.enter_ref = f32[8,256]{1,0:T(8,128)} custom-call(f32[256,256]{1,0:T(8,128)} %get-tuple-element.17.map_ref, f32[8,256]{1,0:T(8,128)} %get-tuple-element.22.shift_ref, f32[8,256]{1,0:T(8,128)} %broadcast_in_dim.20.first_ref), custom_call_target="tpu_custom_call" | custom-call | tf_op jit(solution)/shard_map/pallas_call | solution.py:209
  128.0 12.2 %shard_map.90 = (f32[1,64,256]{2,1,0:T(8,128)}, f32[256,256]{1,0:T(8,128)}) custom-call(f32[8,8,256,256]{3,2,1,0:T(8,128)} %bitcast.8, f32[8,256,256]{2,1,0:T(8,128)} %get-tuple-element.16.pmap_ref, f32[8,256]{1,0:T(8,128)} %shard_map.89.enter_ref, f32[8,256]{1,0:T(8,128)} %get-tuple-element.23.carried_ref, f32[8,8,256]{2,1,0:T(8,128)} %get-tuple-element.24.filtered_ref, ...), custom_call_target="tpu_custom_call" | custom-call | tf_op jit(solution)/shard_map/pallas_call | solution.py:413
  140.2 19.6 %shard_map.91 = f32[4,8,8,256]{3,2,1,0:T(8,128)} custom-call(f32[4,8,8,256]{3,2,1,0:T(8,128)} %bitcast.10), custom_call_target="tpu_custom_call" | custom-call | tf_op jit(solution)/shard_map/pallas_call | solution.py:368
  159.8 1.7 %copy.12 = f32[256,256]{1,0:T(8,128)} copy(f32[256,256]{1,0:T(8,128)} %bitcast.9) | data formatting | bytes 524288
Async XLA Ops:
  0.6 56.0 %copy-start = (f32[1,256]{1,0:T(1,128)S(1)}, f32[1,256]{1,0:T(1,128)}, u32[]{:S(2)}) copy-start(f32[1,256]{1,0:T(1,128)} %param.11) | copy-start | bytes 3076

commit v3 on v0

v3 whole, which is shorter than its diff:
```python
import functools

import jax
import jax.numpy as jnp
from jax import lax
from jax.experimental import pallas as pl
from jax.experimental.pallas import tpu as pltpu
from jax.sharding import PartitionSpec as P

HIGHEST = lax.Precision.HIGHEST
LANES = 128
SUB = 8
CHUNKS = 8
GROUP = 2
PACE = 16
VMEM_BYTES = 60 * 1024 * 1024


def split(x):
    high = x.astype(jnp.bfloat16)
    low = (x - high.astype(jnp.float32)).astype(jnp.bfloat16)
    return high, low


def dot_rhs_t(a, b):
    return lax.dot_general(a, b, (((1,), (1,)), ((), ())), preferred_element_type=jnp.float32)


def to_column(row):
    width = row.shape[1]
    padded = jnp.concatenate([row, jnp.zeros((LANES - SUB, width), jnp.float32)], axis=0)
    return padded.T


def estimate_kernel(count, pace, pattern_ref, trans_ref, obs_ref, meas_ref, fgain_ref, sgain_ref, prior_ref,
                    smoothed_ref, info_ref,
                    dense, rest_high, rest_low, diagonals, gains, drives, fmaps, shifts, smaps, prefix, prefix_shift,
                    filtered, change, out_f, in_f, out_s, in_s, load_sem, send_sem, recv_sem):
    me = lax.axis_index("tm")
    chunks, length, width, _ = dense.shape
    blocks = pattern_ref.shape[1]
    block = width // blocks
    groups = chunks // GROUP
    f32 = jnp.float32
    barrier = pltpu.get_barrier_semaphore()

    @pl.when(me > 0)
    def _():
        pl.semaphore_signal(barrier, inc=1, device_id={"tm": me - 1})

    @pl.when(me < count - 1)
    def _():
        pl.semaphore_signal(barrier, inc=1, device_id={"tm": me + 1})

    def load(j):
        return pltpu.make_async_copy(trans_ref.at[:, j], dense.at[:, j], load_sem.at[j])

    for j in range(length):
        load(j).start()
    fgain, sgain = fgain_ref[...], sgain_ref[...]
    lane = lax.broadcasted_iota(jnp.int32, (1, width), 1) // block
    on_diagonal = (lax.broadcasted_iota(jnp.int32, (width, width), 0)
                   == lax.broadcasted_iota(jnp.int32, (width, width), 1))

    def gains_of(c, j):
        t = c * length + j
        gain = fgain * obs_ref[0, pl.ds(t, 1), :].astype(f32)
        drive = gain * meas_ref[0, pl.ds(t, 1), :]
        gains[j, pl.ds(c, 1), :] = gain
        drives[j, pl.ds(c, 1), :] = drive
        return 1.0 - gain, drive

    def masked(c, j):
        t = c * length + j
        pieces = []
        for i in range(blocks):
            weights = jnp.zeros((1, width), f32)
            for k in range(blocks):
                weights = jnp.where(lane == k, pattern_ref[t, i, k].astype(f32), weights)
            pieces.append(dense[c, j, i * block:(i + 1) * block, :] * weights)
        value = jnp.concatenate(pieces, axis=0)
        dense[c, j] = value
        return value

    def propagate(rows, diagonal, right_high, right_low):
        high, low = split(rows)
        left = jnp.concatenate([high, low, high], axis=1)
        right = jnp.concatenate([right_high, right_high, right_low], axis=1)
        return rows * diagonal + dot_rhs_t(left, right)

    load(0).wait()

    def first_step(c, _):
        keep, drive = gains_of(c, 0)
        turned = masked(c, 0).T
        fmaps[c] = turned * keep
        smaps[c] = turned * sgain
        shifts[c] = jnp.broadcast_to(drive, (2 * SUB, width))
        return 0

    lax.fori_loop(0, chunks, first_step, 0)

    def filter_step(j, _):
        load(j).wait()

        def group_step(g, _):
            for k in range(GROUP):
                c = g * GROUP + k
                keep, drive = gains_of(c, j)
                value = masked(c, j)
                diagonal = jnp.sum(jnp.where(on_diagonal, value, 0.0), axis=0, keepdims=True)
                high, low = split(jnp.where(on_diagonal, 0.0, value))
                diagonals[c, pl.ds(j, 1), :] = diagonal
                rest_high[c, j] = high
                rest_low[c, j] = low
                moved = propagate(jnp.concatenate([fmaps[c], shifts[c]], axis=0), diagonal, high, low)
                fmaps[c] = moved[0:width] * keep
                shifts[c] = moved[width:] * keep + drive
            return 0

        return lax.fori_loop(0, groups, group_step, 0)

    lax.fori_loop(1, length, filter_step, 0)

    prefix[0] = fmaps[0]
    prefix_shift[0] = shifts[0]

    def join(c, _):
        prefix[c] = jnp.dot(prefix[c - 1], fmaps[c], precision=HIGHEST)
        prefix_shift[c] = jnp.dot(prefix_shift[c - 1], fmaps[c], precision=HIGHEST) + shifts[c]
        return 0

    lax.fori_loop(1, chunks, join, 0)

    def smoother_unit(u, _):
        j, g = 1 + u // groups, lax.rem(u, groups)
        for k in range(GROUP):
            c = g * GROUP + k
            smaps[c] = sgain * propagate(smaps[c], diagonals[c, pl.ds(j, 1), :], rest_high[c, j], rest_low[c, j])
        return 0

    units = (length - 1) * groups
    before = jnp.minimum(units, (me * pace) // 8)
    lax.fori_loop(0, before, smoother_unit, 0)

    ends = (me == 0) | (me == count - 1)

    @pl.when(ends)
    def _():
        pl.semaphore_wait(barrier, 1)

    @pl.when(jnp.logical_not(ends))
    def _():
        pl.semaphore_wait(barrier, 2)

    def forward_copy(peer):
        return pltpu.make_async_remote_copy(
            src_ref=out_f, dst_ref=in_f, send_sem=send_sem.at[0], recv_sem=recv_sem.at[0], device_id={"tm": peer})

    def backward_copy(peer):
        return pltpu.make_async_remote_copy(
            src_ref=out_s, dst_ref=in_s, send_sem=send_sem.at[1], recv_sem=recv_sem.at[1], device_id={"tm": peer})

    start_row = jnp.broadcast_to(prior_ref[...], (SUB, width))

    @pl.when(me > 0)
    def _():
        forward_copy(me - 1).wait_recv()
        filtered[0] = in_f[...]

    @pl.when(me == 0)
    def _():
        filtered[0] = start_row

    start = filtered[0]
    column = to_column(start)[:, 0:1]

    @pl.when(me < count - 1)
    def _():
        moved = jnp.sum(prefix[chunks - 1] * column, axis=0, keepdims=True)
        out_f[...] = jnp.broadcast_to(moved, (SUB, width)) + prefix_shift[chunks - 1, 0:SUB, :]
        forward_copy(me + 1).start()

    lax.fori_loop(before, units, smoother_unit, 0)

    rows = [start[0:1]]
    for c in range(chunks - 1):
        rows.append(prefix_shift[c, 0:1, :] + jnp.sum(prefix[c] * column, axis=0, keepdims=True))
    states = jnp.concatenate(rows, axis=0)
    spot = lax.broadcasted_iota(jnp.int32, (width, LANES), 1)

    def forward(j, state):
        gathered = jnp.zeros((width, LANES), f32)
        for c in range(chunks):
            moved = jnp.sum(dense[c, j] * state[c:c + 1, :], axis=1, keepdims=True)
            gathered = jnp.where(spot == c, moved, gathered)
        predict = gathered.T[0:chunks]
        new = (1.0 - gains[j]) * predict + drives[j]
        filtered[j] = new
        change[j] = new - predict
        return new

    lax.fori_loop(0, length, forward, states)

    prefix[0] = smaps[0]

    def join_smoother(c, _):
        prefix[0] = jnp.dot(prefix[0], smaps[c], precision=HIGHEST)
        return 0

    lax.fori_loop(1, chunks, join_smoother, 0)

    def turned_step(j, values):
        columns = to_column(values)
        return jnp.concatenate([
            jnp.sum(dense[c, j] * columns[:, c:c + 1], axis=0, keepdims=True) for c in range(chunks)
        ], axis=0)

    def backward(i, carried):
        j = length - 1 - i
        return turned_step(j, change[j] + sgain * carried)

    carried = lax.fori_loop(0, length, backward, jnp.zeros((chunks, width), f32))

    def lowered(table, row):
        moved = jnp.sum(table * row, axis=1, keepdims=True)
        return jnp.broadcast_to(moved, (width, LANES)).T[0:1]

    shift = carried[chunks - 1:chunks]
    for c in range(chunks - 2, -1, -1):
        shift = carried[c:c + 1] + lowered(smaps[c], shift)

    @pl.when(me < count - 1)
    def _():
        backward_copy(me + 1).wait_recv()

    @pl.when(me == count - 1)
    def _():
        in_s[...] = jnp.zeros_like(in_s)

    entering = in_s[0:1, :]

    @pl.when(me > 0)
    def _():
        out_s[...] = jnp.broadcast_to(shift + lowered(prefix[0], entering), (SUB, width))
        backward_copy(me - 1).start()

    rows = [entering]
    for c in range(chunks - 1, 0, -1):
        rows.insert(0, carried[c:c + 1] + lowered(smaps[c], rows[0]))

    def final(i, carry):
        j = length - 1 - i
        lifted = sgain * carry
        smoothed = filtered[j] + lifted
        for c in range(chunks):
            smoothed_ref[0, pl.ds(c * length + j, 1), :] = smoothed[c:c + 1]
        residual = change[j] + lifted
        filtered[j] = residual
        return turned_step(j, residual)

    lax.fori_loop(0, length, final, jnp.concatenate(rows, axis=0))
    every = filtered[...].reshape(length * chunks, width)
    info_ref[...] = lax.dot_general(
        every, every, (((0,), (0,)), ((), ())), precision=HIGHEST, preferred_element_type=f32)

    @pl.when(me < count - 1)
    def _():
        forward_copy(me + 1).wait_send()

    @pl.when(me > 0)
    def _():
        backward_copy(me - 1).wait_send()


def total_kernel(parts, blocks, scale, local_ref, out_ref, part, box_e, box_t, send_sem, recv_sem):
    e, t = lax.axis_index("exp"), lax.axis_index("tm")
    barrier = pltpu.get_barrier_semaphore()
    e_peers = [lax.rem(e + k, parts) for k in range(1, parts)]
    t_peers = [lax.rem(t + k, blocks) for k in range(1, blocks)]
    for peer in e_peers:
        pl.semaphore_signal(barrier, inc=1, device_id={"exp": peer})
    for peer in t_peers:
        pl.semaphore_signal(barrier, inc=1, device_id={"tm": peer})
    pl.semaphore_wait(barrier, parts + blocks - 2)

    def send(src, dst, number, device):
        copy = pltpu.make_async_remote_copy(
            src_ref=src, dst_ref=dst, send_sem=send_sem.at[number], recv_sem=recv_sem.at[number],
            device_id=device)
        copy.start()
        return copy

    first = [send(local_ref.at[p], box_e.at[k], k, {"exp": p}) for k, p in enumerate(e_peers)]
    base = len(first)
    value = local_ref[e]
    for k, copy in enumerate(first):
        copy.wait_recv()
        value = value + box_e[k]
    part[...] = value
    second = [send(part.at[p], box_t.at[k], base + k, {"tm": p}) for k, p in enumerate(t_peers)]
    base += len(second)
    mine = part[t]
    for k, copy in enumerate(second):
        copy.wait_recv()
        mine = mine + box_t[k]
    out_ref[e, t] = mine * scale
    third = [send(out_ref.at[e, t], out_ref.at[e, t], base + k, {"tm": p}) for k, p in enumerate(t_peers)]
    base += len(third)
    for k, copy in enumerate(third):
        sender = lax.rem(t + blocks - 1 - k, blocks)
        pltpu.make_async_remote_copy(
            src_ref=out_ref.at[e, sender], dst_ref=out_ref.at[e, sender], send_sem=send_sem.at[base - len(third) + k],
            recv_sem=recv_sem.at[base - len(third) + k], device_id={"tm": sender}).wait_recv()
    fourth = [send(out_ref.at[e], out_ref.at[e], base + k, {"exp": p}) for k, p in enumerate(e_peers)]
    for k, copy in enumerate(fourth):
        sender = lax.rem(e + parts - 1 - k, parts)
        pltpu.make_async_remote_copy(
            src_ref=out_ref.at[sender], dst_ref=out_ref.at[sender], send_sem=send_sem.at[base + k],
            recv_sem=recv_sem.at[base + k], device_id={"exp": sender}).wait_recv()
    for copy in first + second + third + fourth:
        copy.wait_send()


def total(local, scale, ident):
    parts, blocks = lax.axis_size("exp"), lax.axis_size("tm")
    width = local.shape[0]
    rows = width // (parts * blocks)
    copies = 2 * (parts - 1) + 2 * (blocks - 1)
    f32 = jnp.float32
    vmem = pl.BlockSpec(memory_space=pltpu.VMEM)
    summed = pl.pallas_call(
        functools.partial(total_kernel, parts, blocks, scale),
        in_specs=[vmem],
        out_specs=vmem,
        out_shape=jax.ShapeDtypeStruct((parts, blocks, rows, width), f32),
        scratch_shapes=[
            pltpu.VMEM((blocks, rows, width), f32),
            pltpu.VMEM((parts - 1, blocks, rows, width), f32),
            pltpu.VMEM((blocks - 1, rows, width), f32),
            pltpu.SemaphoreType.DMA((copies,)),
            pltpu.SemaphoreType.DMA((copies,)),
        ],
        compiler_params=pltpu.CompilerParams(collective_id=ident, has_side_effects=True),
    )(local.reshape(parts, blocks, rows, width))
    return summed.reshape(width, width)


def shards(transitions, pattern, obs_mask, measured, prior_mean, filter_gain, smooth_gain):
    steps, width, _ = transitions.shape
    length = steps // CHUNKS
    f32 = jnp.float32
    vmem = pl.BlockSpec(memory_space=pltpu.VMEM)
    row = pltpu.VMEM((SUB, width), f32)
    square = (CHUNKS, width, width)
    by_step = pltpu.VMEM((length, CHUNKS, width), f32)
    smoothed, local_info = pl.pallas_call(
        functools.partial(estimate_kernel, lax.axis_size("tm"), PACE),
        in_specs=[pl.BlockSpec(memory_space=pltpu.SMEM), pl.BlockSpec(memory_space=pl.ANY)] + [vmem] * 5,
        out_specs=[vmem] * 2,
        out_shape=[jax.ShapeDtypeStruct((1, steps, width), f32), jax.ShapeDtypeStruct((width, width), f32)],
        scratch_shapes=[
            pltpu.VMEM((CHUNKS, length, width, width), f32),
            pltpu.VMEM((CHUNKS, length, width, width), jnp.bfloat16),
            pltpu.VMEM((CHUNKS, length, width, width), jnp.bfloat16),
            pltpu.VMEM((CHUNKS, length, width), f32),
            by_step,
            by_step,
            pltpu.VMEM(square, f32),
            pltpu.VMEM((CHUNKS, 2 * SUB, width), f32),
            pltpu.VMEM(square, f32),
            pltpu.VMEM(square, f32),
            pltpu.VMEM((CHUNKS, 2 * SUB, width), f32),
            by_step,
            by_step,
            row, row, row, row,
            pltpu.SemaphoreType.DMA((length,)),
            pltpu.SemaphoreType.DMA((2,)),
            pltpu.SemaphoreType.DMA((2,)),
        ],
        compiler_params=pltpu.CompilerParams(
            vmem_limit_bytes=VMEM_BYTES, collective_id=0, has_side_effects=True),
    )(pattern, transitions.reshape(CHUNKS, length, width, width), obs_mask, measured,
      filter_gain[None, :], smooth_gain[None, :], prior_mean)
    scale = 1.0 / (steps * lax.axis_size("tm") * lax.axis_size("exp"))
    return smoothed, total(local_info, scale, 1)


def solution(mesh):
    in_specs = (
        P("tm", None, None),
        P("tm", None, None),
        P("exp", "tm", None),
        P("exp", "tm", None),
        P("exp", None),
        P(),
        P(),
    )
    out_specs = (P("exp", "tm", None), P())
    return jax.shard_map(shards, mesh=mesh, in_specs=in_specs, out_specs=out_specs, check_vma=False)
```

time: 676 us -> 116 us (0.17); the launches traced: 666 us -> 116 us
  matrix products: 383 us -> 0 us
  waiting for transfers between devices: 124 us -> 0 us
  Pallas kernels: 0 us -> 111 us
  local copies, waits for them, and re-layouts: 63 us -> 4.61 us
  blocking collectives: 38.6 us -> 0 us
  other arithmetic: 33 us -> 0 us
  between operations: 14 us -> 0.65 us
  loops' own time: 9.82 us -> 0 us
    dot_general x294 -> x0, matrix products: 383 us -> none  [the longest x128 157 us: update(): predict = jnp.dot(trans_step, state, precision=lax.Precision.HIGHEST)]
    psum x1 -> x0, waiting for transfers between devices: 124 us -> none  [shards(): total_info = lax.psum(local_info, ('tm', 'exp'))]
    pallas_call x0 -> x2, Pallas kernels: none -> 111 us  [the longest x1 89.8 us: shards(): pl.pallas_call(functools.partial(estimate_kernel, lax.axis_size('tm'), PA...]
    mul x2 -> x0, local copies, waits for them, and re-layouts: 41.7 us -> none  [masked_dense(): return (reshaped * weights).reshape(count_steps, state_width, state_width)]
    all_gather x2 -> x0, blocking collectives: 38.6 us -> none  [entering(): everything = jax.tree.map(lambda part: lax.all_gather(part, axis), x)]
    mul x3 -> x0, other arithmetic: 25 us -> none  [the longest x1 17.7 us: shards(): filter_map = chain_product(keep_rows[:, :, None] * dense_steps)]
    dynamic_update_slice x256 -> x0, local copies, waits for them, and re-layouts: 12.1 us -> none  [run_filter(): lax.scan(update, start_state, (dense_steps, keep_rows, drive_terms))]
    another operation x6 -> x0, loops' own time: 9.82 us -> none  [the longest x2 5.2 us: run_filter(): lax.scan(update, start_state, (dense_steps, keep_rows, drive_terms))]
  transfers between devices with their start and end apart: 3 -> 0, of which waited for: 1 -> 0; matrix products, arithmetic and copies ran while one was open for 45% -> 0% of each run, Pallas kernels for 0% -> 0%
where the time goes in v3:
time: 116 us
  Pallas kernels  111 us (96%)
  local copies, waits for them, and re-layouts  4.61 us (4%)
    pallas_call x1, Pallas kernels, shards(): pl.pallas_call(functools.partial(estimate_kernel, lax.axis_size('tm'), PA...  89.8 us
    pallas_call x1, Pallas kernels, total(): pl.pallas_call(functools.partial(total_kernel, parts, blocks, scale), in_...  20.9 us
    unnamed x3, local copies, waits for them, and re-layouts  4.61 us

profile of v3, /device:TPU:0, one launch (start us, length us, event | category | flops | bytes accessed | tf_op | source)
XLA Modules:
  0.0 115.9 jit_solution(6622587816792431984)
XLA Ops:
  0.6 1.5 %copy.9.pattern_ref = s32[64,4,4]{2,1,0:T(4,128)} copy(s32[64,4,4]{0,2,1:T(4,128)} %param.8) | data formatting | bytes 8192 | tf_op args[1]
  2.1 89.8 %shard_map.86 = (f32[1,64,256]{2,1,0:T(8,128)}, f32[256,256]{1,0:T(8,128)}) custom-call(s32[64,4,4]{2,1,0:T(4,128)} %copy.9.pattern_ref, f32[8,8,256,256]{3,2,1,0:T(8,128)} %bitcast.5, s32[1,64,256]{2,1,0:T(8,128)} %obs_ref.1, f32[1,64,256]{2,1,0:T(8,128)} %meas_ref.1, f32[1,256]{1,0:T(1,128)} %bitcast.8, f32[1,256]{1,0:T(1,128)} %bitcast.9, f32[1,256]{1,0:T(1,128)} %prior_ref.1), custom_call_target="tpu_custom_call" | custom-call | tf_op jit(solution)/shard_map/pallas_call | solution.py:357
  91.9 20.9 %shard_map.87 = f32[4,8,8,256]{3,2,1,0:T(8,128)} custom-call(f32[4,8,8,256]{3,2,1,0:T(8,128)} %bitcast.7), custom_call_target="tpu_custom_call" | custom-call | tf_op jit(solution)/shard_map/pallas_call | solution.py:332
  112.7 1.5 %copy.12 = f32[1,64,256]{2,1,0:T(8,128)} copy(f32[1,64,256]{2,1,0:T(8,128)} %get-tuple-element.8) | data formatting | bytes 131072
  114.2 1.7 %copy.13 = f32[256,256]{1,0:T(8,128)} copy(f32[256,256]{1,0:T(8,128)} %bitcast.6) | data formatting | bytes 524288

commit v4 on v3

--- a/solution.py
+++ b/solution.py
@@ -11,7 +11,7 @@
 LANES = 128
 SUB = 8
 CHUNKS = 8
-GROUP = 2
+GROUP = 4
 PACE = 16
 VMEM_BYTES = 60 * 1024 * 1024
 
@@ -32,10 +32,11 @@
     return padded.T
 
 
-def estimate_kernel(count, pace, pattern_ref, trans_ref, obs_ref, meas_ref, fgain_ref, sgain_ref, prior_ref,
+def estimate_kernel(parts, count, pace, scale, pattern_ref, trans_ref, obs_ref, meas_ref, fgain_ref, sgain_ref, prior_ref,
                     smoothed_ref, info_ref,
                     dense, rest_high, rest_low, diagonals, gains, drives, fmaps, shifts, smaps, prefix, prefix_shift,
-                    filtered, change, out_f, in_f, out_s, in_s, load_sem, send_sem, recv_sem):
+                    filtered, change, out_f, in_f, out_s, in_s, local, part, box_e, box_t,
+                    whole_map, load_sem, send_sem, recv_sem, total_send, total_recv):
     me = lax.axis_index("tm")
     chunks, length, width, _ = dense.shape
     blocks = pattern_ref.shape[1]
@@ -44,13 +45,13 @@
     f32 = jnp.float32
     barrier = pltpu.get_barrier_semaphore()
 
-    @pl.when(me > 0)
-    def _():
-        pl.semaphore_signal(barrier, inc=1, device_id={"tm": me - 1})
-
-    @pl.when(me < count - 1)
-    def _():
-        pl.semaphore_signal(barrier, inc=1, device_id={"tm": me + 1})
+    part_at = lax.axis_index("exp")
+    e_peers = [lax.rem(part_at + k, parts) for k in range(1, parts)]
+    t_peers = [lax.rem(me + k, count) for k in range(1, count)]
+    for peer in e_peers:
+        pl.semaphore_signal(barrier, inc=1, device_id={"exp": peer})
+    for peer in t_peers:
+        pl.semaphore_signal(barrier, inc=1, device_id={"tm": peer})
 
     def load(j):
         return pltpu.make_async_copy(trans_ref.at[:, j], dense.at[:, j], load_sem.at[j])
@@ -143,15 +144,21 @@
     before = jnp.minimum(units, (me * pace) // 8)
     lax.fori_loop(0, before, smoother_unit, 0)
 
-    ends = (me == 0) | (me == count - 1)
-
-    @pl.when(ends)
-    def _():
-        pl.semaphore_wait(barrier, 1)
-
-    @pl.when(jnp.logical_not(ends))
-    def _():
-        pl.semaphore_wait(barrier, 2)
+    def join_smoother(c, _):
+        whole_map[...] = jnp.dot(whole_map[...], smaps[c], precision=HIGHEST)
+        return 0
+
+    def join_all():
+        whole_map[...] = smaps[0]
+        lax.fori_loop(1, chunks, join_smoother, 0)
+
+    early = before == units
+
+    @pl.when(early)
+    def _():
+        join_all()
+
+    pl.semaphore_wait(barrier, parts + count - 2)
 
     def forward_copy(peer):
         return pltpu.make_async_remote_copy(
@@ -202,13 +209,9 @@
 
     lax.fori_loop(0, length, forward, states)
 
-    prefix[0] = smaps[0]
-
-    def join_smoother(c, _):
-        prefix[0] = jnp.dot(prefix[0], smaps[c], precision=HIGHEST)
-        return 0
-
-    lax.fori_loop(1, chunks, join_smoother, 0)
+    @pl.when(jnp.logical_not(early))
+    def _():
+        join_all()
 
     def turned_step(j, values):
         columns = to_column(values)
@@ -242,7 +245,7 @@
 
     @pl.when(me > 0)
     def _():
-        out_s[...] = jnp.broadcast_to(shift + lowered(prefix[0], entering), (SUB, width))
+        out_s[...] = jnp.broadcast_to(shift + lowered(whole_map[...], entering), (SUB, width))
         backward_copy(me - 1).start()
 
     rows = [entering]
@@ -261,8 +264,10 @@
 
     lax.fori_loop(0, length, final, jnp.concatenate(rows, axis=0))
     every = filtered[...].reshape(length * chunks, width)
-    info_ref[...] = lax.dot_general(
-        every, every, (((0,), (0,)), ((), ())), precision=HIGHEST, preferred_element_type=f32)
+    local[...] = lax.dot_general(
+        every, every, (((0,), (0,)), ((), ())), precision=HIGHEST, preferred_element_type=f32,
+    ).reshape(local.shape)
+    add_up(part_at, me, e_peers, t_peers, scale, local, info_ref, part, box_e, box_t, total_send, total_recv)
 
     @pl.when(me < count - 1)
     def _():
@@ -273,16 +278,8 @@
         backward_copy(me - 1).wait_send()
 
 
-def total_kernel(parts, blocks, scale, local_ref, out_ref, part, box_e, box_t, send_sem, recv_sem):
-    e, t = lax.axis_index("exp"), lax.axis_index("tm")
-    barrier = pltpu.get_barrier_semaphore()
-    e_peers = [lax.rem(e + k, parts) for k in range(1, parts)]
-    t_peers = [lax.rem(t + k, blocks) for k in range(1, blocks)]
-    for peer in e_peers:
-        pl.semaphore_signal(barrier, inc=1, device_id={"exp": peer})
-    for peer in t_peers:
-        pl.semaphore_signal(barrier, inc=1, device_id={"tm": peer})
-    pl.semaphore_wait(barrier, parts + blocks - 2)
+def add_up(e, t, e_peers, t_peers, scale, local_ref, out_ref, part, box_e, box_t, send_sem, recv_sem):
+    parts, blocks = len(e_peers) + 1, len(t_peers) + 1
 
     def send(src, dst, number, device):
         copy = pltpu.make_async_remote_copy(
@@ -322,30 +319,6 @@
         copy.wait_send()
 
 
-def total(local, scale, ident):
-    parts, blocks = lax.axis_size("exp"), lax.axis_size("tm")
-    width = local.shape[0]
-    rows = width // (parts * blocks)
-    copies = 2 * (parts - 1) + 2 * (blocks - 1)
-    f32 = jnp.float32
-    vmem = pl.BlockSpec(memory_space=pltpu.VMEM)
-    summed = pl.pallas_call(
-        functools.partial(total_kernel, parts, blocks, scale),
-        in_specs=[vmem],
-        out_specs=vmem,
-        out_shape=jax.ShapeDtypeStruct((parts, blocks, rows, width), f32),
-        scratch_shapes=[
-            pltpu.VMEM((blocks, rows, width), f32),
-            pltpu.VMEM((parts - 1, blocks, rows, width), f32),
-            pltpu.VMEM((blocks - 1, rows, width), f32),
-            pltpu.SemaphoreType.DMA((copies,)),
-            pltpu.SemaphoreType.DMA((copies,)),
-        ],
-        compiler_params=pltpu.CompilerParams(collective_id=ident, has_side_effects=True),
-    )(local.reshape(parts, blocks, rows, width))
-    return summed.reshape(width, width)
-
-
 def shards(transitions, pattern, obs_mask, measured, prior_mean, filter_gain, smooth_gain):
     steps, width, _ = transitions.shape
     length = steps // CHUNKS
@@ -354,11 +327,15 @@
     row = pltpu.VMEM((SUB, width), f32)
     square = (CHUNKS, width, width)
     by_step = pltpu.VMEM((length, CHUNKS, width), f32)
-    smoothed, local_info = pl.pallas_call(
-        functools.partial(estimate_kernel, lax.axis_size("tm"), PACE),
+    parts, blocks = lax.axis_size("exp"), lax.axis_size("tm")
+    rows = width // (parts * blocks)
+    scale = 1.0 / (steps * blocks * parts)
+    copies = 2 * (parts + blocks - 2)
+    smoothed, information = pl.pallas_call(
+        functools.partial(estimate_kernel, parts, blocks, PACE, scale),
         in_specs=[pl.BlockSpec(memory_space=pltpu.SMEM), pl.BlockSpec(memory_space=pl.ANY)] + [vmem] * 5,
         out_specs=[vmem] * 2,
-        out_shape=[jax.ShapeDtypeStruct((1, steps, width), f32), jax.ShapeDtypeStruct((width, width), f32)],
+        out_shape=[jax.ShapeDtypeStruct((1, steps, width), f32), jax.ShapeDtypeStruct((parts, blocks, rows, width), f32)],
         scratch_shapes=[
             pltpu.VMEM((CHUNKS, length, width, width), f32),
             pltpu.VMEM((CHUNKS, length, width, width), jnp.bfloat16),
@@ -374,16 +351,22 @@
             by_step,
             by_step,
             row, row, row, row,
+            pltpu.VMEM((parts, blocks, rows, width), f32),
+            pltpu.VMEM((blocks, rows, width), f32),
+            pltpu.VMEM((parts - 1, blocks, rows, width), f32),
+            pltpu.VMEM((blocks - 1, rows, width), f32),
+            pltpu.VMEM((width, width), f32),
             pltpu.SemaphoreType.DMA((length,)),
             pltpu.SemaphoreType.DMA((2,)),
             pltpu.SemaphoreType.DMA((2,)),
+            pltpu.SemaphoreType.DMA((copies,)),
+            pltpu.SemaphoreType.DMA((copies,)),
         ],
         compiler_params=pltpu.CompilerParams(
             vmem_limit_bytes=VMEM_BYTES, collective_id=0, has_side_effects=True),
     )(pattern, transitions.reshape(CHUNKS, length, width, width), obs_mask, measured,
       filter_gain[None, :], smooth_gain[None, :], prior_mean)
-    scale = 1.0 / (steps * lax.axis_size("tm") * lax.axis_size("exp"))
-    return smoothed, total(local_info, scale, 1)
+    return smoothed, information.reshape(width, width)
 
 
 def solution(mesh):

time: 116 us -> 102 us (0.88)
  Pallas kernels: 111 us -> 96.3 us
    pallas_call x2 -> x1, Pallas kernels: 111 us -> 96.3 us  [shards(): pl.pallas_call(functools.partial(estimate_kernel, parts, blocks, PACE, sc...]
where the time goes in v4:
time: 102 us
  Pallas kernels  96.3 us (94%)
  local copies, waits for them, and re-layouts  4.61 us (5%)
    pallas_call x1, Pallas kernels, shards(): pl.pallas_call(functools.partial(estimate_kernel, parts, blocks, PACE, sc...  96.3 us
    unnamed x3, local copies, waits for them, and re-layouts  4.61 us

profile of v4, /device:TPU:0, one launch (start us, length us, event | category | flops | bytes accessed | tf_op | source)
XLA Modules:
  0.0 101.5 jit_solution(1929102386986077896)
XLA Ops:
  0.6 1.5 %copy.9.pattern_ref = s32[64,4,4]{2,1,0:T(4,128)} copy(s32[64,4,4]{0,2,1:T(4,128)} %param.8) | data formatting | bytes 8192 | tf_op args[1]
  2.1 96.3 %shard_map.86 = (f32[1,64,256]{2,1,0:T(8,128)}, f32[4,8,8,256]{3,2,1,0:T(8,128)}) custom-call(s32[64,4,4]{2,1,0:T(4,128)} %copy.9.pattern_ref, f32[8,8,256,256]{3,2,1,0:T(8,128)} %bitcast.4, s32[1,64,256]{2,1,0:T(8,128)} %obs_ref.1, f32[1,64,256]{2,1,0:T(8,128)} %meas_ref.1, f32[1,256]{1,0:T(1,128)} %bitcast.6, f32[1,256]{1,0:T(1,128)} %bitcast.7, ...), custom_call_target="tpu_custom_call" | custom-call | tf_op jit(solution)/shard_map/pallas_call | solution.py:334
  98.4 1.5 %copy.12 = f32[1,64,256]{2,1,0:T(8,128)} copy(f32[1,64,256]{2,1,0:T(8,128)} %get-tuple-element.8) | data formatting | bytes 131072
  99.8 1.7 %copy.13 = f32[256,256]{1,0:T(8,128)} copy(f32[256,256]{1,0:T(8,128)} %bitcast.5) | data formatting | bytes 524288

commit v5 on v4

--- a/solution.py
+++ b/solution.py
@@ -11,7 +11,7 @@
 LANES = 128
 SUB = 8
 CHUNKS = 8
-GROUP = 4
+GROUP = 8
 PACE = 16
 VMEM_BYTES = 60 * 1024 * 1024
 

time: 102 us -> 101 us (level)
  no operation moved by 1% of the time
where the time goes in v5:
time: 101 us
  Pallas kernels  95.4 us (94%)
  local copies, waits for them, and re-layouts  4.61 us (5%)
    pallas_call x1, Pallas kernels, shards(): pl.pallas_call(functools.partial(estimate_kernel, parts, blocks, PACE, sc...  95.4 us
    unnamed x3, local copies, waits for them, and re-layouts  4.61 us

profile of v5, /device:TPU:0, one launch (start us, length us, event | category | flops | bytes accessed | tf_op | source)
XLA Modules:
  0.0 100.7 jit_solution(17316699325152038235)
XLA Ops:
  0.6 1.5 %copy.9.pattern_ref = s32[64,4,4]{2,1,0:T(4,128)} copy(s32[64,4,4]{0,2,1:T(4,128)} %param.8) | data formatting | bytes 8192 | tf_op args[1]
  2.1 95.4 %shard_map.86 = (f32[1,64,256]{2,1,0:T(8,128)}, f32[4,8,8,256]{3,2,1,0:T(8,128)}) custom-call(s32[64,4,4]{2,1,0:T(4,128)} %copy.9.pattern_ref, f32[8,8,256,256]{3,2,1,0:T(8,128)} %bitcast.4, s32[1,64,256]{2,1,0:T(8,128)} %obs_ref.1, f32[1,64,256]{2,1,0:T(8,128)} %meas_ref.1, f32[1,256]{1,0:T(1,128)} %bitcast.6, f32[1,256]{1,0:T(1,128)} %bitcast.7, ...), custom_call_target="tpu_custom_call" | custom-call | tf_op jit(solution)/shard_map/pallas_call | solution.py:334
  97.5 1.5 %copy.12 = f32[1,64,256]{2,1,0:T(8,128)} copy(f32[1,64,256]{2,1,0:T(8,128)} %get-tuple-element.8) | data formatting | bytes 131072
  99.0 1.7 %copy.13 = f32[256,256]{1,0:T(8,128)} copy(f32[256,256]{1,0:T(8,128)} %bitcast.5) | data formatting | bytes 524288
